TPU v7x, 32 devices: a whole 2x2x4 slice. The times are simulated.
32 devices in a mesh: pair: 8 (over z, x), row: 4 (over y, core).
Axes of the slice: x: 2, y: 2, z: 4, core: 2. Of those that a mesh axis runs over, the one named last changes fastest.
Arguments:
- sector: float32 [8192, 2048], P('row', 'pair'), may hold values from -1.767767 to 1.767767
- block_label: int32 [16], replicated, may hold values from 0 to 15, each once
Outputs:
- rotated: float32 [8192, 2048], P('row', 'pair')
- vectors: float32 [2048, 2048], P('row', 'pair')
- singular: float32 [2048], P('pair')
Inputs may be any that keep to these rules, and one draw needn't show every extreme that they name: `block_label`: each block number appears once.
All inputs are finite; a program needn't handle non-finite values.
Results may differ from a plain program's by a relative error of at most 0.0003.
Values sent between devices are 32-bit elements; how exact they have to be, the bound alone decides.
No kernel may reach another device: no remote copies, remote signals or barrier semaphores. Data moves between devices by JAX's collectives and lax.ppermute only.
A program may use at most 64 MiB of HBM per device.

v0:
```python
import jax
import jax.numpy as jnp
from jax import lax
from jax.sharding import PartitionSpec as P

ROUNDS = 4
NEWTON = 16
highest = lax.Precision.HIGHEST


def from_behind(block, axis, distance):
    devices = range(lax.axis_size(axis))
    route = [(i - distance, i) for i in devices if i - distance in devices]
    return lax.ppermute(block, axis, route)


def rotation_of(gram_matrix):
    size_two = gram_matrix.shape[0]
    diagonal = jnp.diagonal(gram_matrix)
    spread = diagonal[None, :] - diagonal[:, None]
    summed = diagonal[None, :] + diagonal[:, None]
    skewed = (
        gram_matrix
        * spread
        / (spread * spread + 2.0 * gram_matrix * gram_matrix + 0.01 * summed * summed)
    )
    identity = jnp.eye(size_two, dtype=jnp.float32)
    half_step = identity + 0.5 * skewed
    system = identity - 0.25 * jnp.dot(skewed, skewed, precision=highest)
    bound = 1.0 + 0.25 * jnp.sum(skewed * skewed)
    inverse = 2.0 / (1.0 + bound) * identity
    for newton_step in range(NEWTON):
        inverse = jnp.dot(
            inverse, 2.0 * identity - jnp.dot(system, inverse, precision=highest), precision=highest
        )
    return jnp.dot(inverse, jnp.dot(half_step, half_step, precision=highest), precision=highest)


def send_leftward(moving):
    return from_behind(moving, "pair", -1)


def send_rightward(moving):
    return from_behind(moving, "pair", 1)


def per_device(sector, block_label):
    local_rows = sector.shape[0]
    width_pair = sector.shape[1]
    half_width = width_pair // 2
    pair_count = lax.axis_size("pair")
    position = lax.axis_index("pair")
    row_index = lax.axis_index("row")
    vector_rows = pair_count * width_pair // lax.axis_size("row")
    labels = lax.dynamic_slice_in_dim(block_label, 2 * position, 2)
    targets = (
        labels[:, None] * half_width + jnp.arange(half_width, dtype=jnp.int32)[None, :]
    ).reshape(width_pair)
    row_ids = row_index * vector_rows + jnp.arange(vector_rows, dtype=jnp.int32)
    vectors = (row_ids[:, None] == targets[None, :]).astype(jnp.float32)
    stacked = jnp.concatenate([sector, vectors], 0)
    is_first = position == 0
    is_last = position == pair_count - 1
    for sweep_round in range(ROUNDS):
        columns = stacked[:local_rows]
        gram_matrix = lax.psum(jnp.dot(columns.T, columns, precision=highest), "row")
        rotation = rotation_of(gram_matrix)
        if sweep_round == ROUNDS - 1:
            stacked = jnp.dot(stacked, rotation, precision=highest)
        else:
            turned = jnp.dot(stacked, rotation, precision=highest)
            upper_half = turned[:, :half_width]
            lower_half = turned[:, half_width:]
            from_right = send_leftward(lower_half)
            from_left = send_rightward(jnp.where(is_first, lower_half, upper_half))
            new_upper = jnp.where(is_first, upper_half, from_left)
            new_lower = jnp.where(is_last, upper_half, from_right)
            stacked = jnp.concatenate([new_upper, new_lower], 1)
    rotated = stacked[:local_rows]
    vectors_out = stacked[local_rows:]
    squares = lax.psum(jnp.sum(rotated * rotated, axis=0), "row")
    singular = jnp.sqrt(squares + 1e-06)
    return (rotated, vectors_out, singular)


def solution(mesh):
    placed = (P("row", "pair"), P())
    return jax.shard_map(
        per_device,
        mesh=mesh,
        in_specs=placed,
        out_specs=(P("row", "pair"), P("row", "pair"), P("pair")),
        check_vma=False,
    )
```

profile of v0, /device:TPU:0, one launch (start us, length us, event | category | flops | bytes accessed | tf_op | source)
XLA Modules:
  0.0 438.3 jit_solution(17083182142614953925)
XLA Ops:
  7.2 6.4 %fusion.107 = f32[256,256]{1,0:T(8,128)} fusion(f32[2048,256]{1,0:T(8,128)} %param.2), kind=kOutput, calls=%fused_computation.216 | convolution fusion | flops 1610612736 | bytes 2359296 | tf_op jit(solution)/shard_map/dot_general | solution.py:66
  14.2 34.3 %all-reduce.5.cloned.1.call-done = f32[256,256]{1,0:T(8,128)} async-done(((f32[256,256]{1,0:T(8,128)}), f32[256,256]{1,0:T(8,128)}) %all-reduce.5.cloned.1.call-update) | async-done | bytes 262160 | tf_op jit(solution)/shard_map/psum | solution.py:66
  48.5 2.6 gather_fusion
  51.1 0.8 multiply_reduce_fusion.4
  52.3 0.4 fusion.56
  63.9 0.6 fusion.120
  66.4 0.4 copy-done
  66.8 2.6 fusion
  69.4 1.7 slice_select_fusion.8
  71.1 4.4 %collective-permute-start = (f32[2560,128]{0,1:T(8,128)}, f32[2560,128]{0,1:T(8,128)}, u32[]{:S(2)}, u32[]{:S(2)}) collective-permute-start(f32[2560,128]{0,1:T(8,128)} %get-tuple-element.23), channel_id=1, source_target_pairs={{0,4},{4,8},{8,12},{12,16},{16,20},{20,24},{24,28},{1,5},{5,9},{9,... | collective-permute-start | bytes 3932168 | tf_op jit(solution)/shard_map/ppermute | solution.py:14
  75.6 1.3 collective-permute-start.1
  76.9 52.9 %collective-permute-done = f32[2560,128]{0,1:T(8,128)} collective-permute-done((f32[2560,128]{0,1:T(8,128)}, f32[2560,128]{0,1:T(8,128)}, u32[]{:S(2)}, u32[]{:S(2)}) %collective-permute-start) | collective-permute-done | bytes 1310752 | tf_op jit(solution)/shard_map/ppermute | solution.py:14
  129.8 1.7 slice_select_fusion.7
  131.5 1.1 copy-done.1
  132.6 0.4 copy-done.3
  133.0 2.6 fusion.24
  135.6 0.4 all-reduce.9.cloned.1.call-start
  136.1 33.4 %all-reduce.7.cloned.1.call-done = f32[256,256]{1,0:T(8,128)} async-done(((f32[256,256]{1,0:T(8,128)}), f32[256,256]{1,0:T(8,128)}) %all-reduce.7.cloned.1.call-update) | async-done | bytes 262160 | tf_op jit(solution)/shard_map/psum | solution.py:66
  169.5 2.6 gather_fusion.1
  172.1 0.8 multiply_reduce_fusion.3
  173.3 0.4 fusion.57
  184.8 0.6 fusion.136
  187.6 2.6 fusion.4
  190.4 3.5 collective-permute-start.2
  193.9 1.3 collective-permute-start.3
  195.2 53.6 %collective-permute-done.2 = f32[2560,128]{0,1:T(8,128)S(1)} collective-permute-done((f32[2560,128]{0,1:T(8,128)S(1)}, f32[2560,128]{0,1:T(8,128)S(1)}, u32[]{:S(2)}, u32[]{:S(2)}) %collective-permute-start.2) | collective-permute-done | bytes 1310752 | tf_op jit(solution)/shard_map/ppermute | solution.py:14
  249.0 2.6 fusion.20
  251.6 0.4 all-reduce.11.cloned.1.call-start
  252.1 33.0 %all-reduce.9.cloned.1.call-done = f32[256,256]{1,0:T(8,128)} async-done(((f32[256,256]{1,0:T(8,128)}), f32[256,256]{1,0:T(8,128)}) %all-reduce.9.cloned.1.call-update) | async-done | bytes 262160 | tf_op jit(solution)/shard_map/psum | solution.py:66
  285.0 2.6 gather_fusion.2
  287.7 0.8 multiply_reduce_fusion.2
  288.9 0.4 fusion.58
  300.4 0.5 fusion.152
  302.9 2.6 fusion.8
  305.7 3.5 collective-permute-start.4
  309.2 1.3 collective-permute-start.5
  310.5 53.6 %collective-permute-done.4 = f32[2560,128]{0,1:T(8,128)S(1)} collective-permute-done((f32[2560,128]{0,1:T(8,128)S(1)}, f32[2560,128]{0,1:T(8,128)S(1)}, u32[]{:S(2)}, u32[]{:S(2)}) %collective-permute-start.4) | collective-permute-done | bytes 1310752 | tf_op jit(solution)/shard_map/ppermute | solution.py:14
  364.3 2.6 fusion.16
  366.9 33.4 %all-reduce.11.cloned.1.call-done = f32[256,256]{1,0:T(8,128)} async-done(((f32[256,256]{1,0:T(8,128)}), f32[256,256]{1,0:T(8,128)}) %all-reduce.11.cloned.1.call-update) | async-done | bytes 262160 | tf_op jit(solution)/shard_map/psum | solution.py:66
  400.4 2.6 gather_fusion.3
  403.0 0.8 multiply_reduce_fusion.1
  404.2 0.4 fusion.59
  413.4 0.6 fusion.165
  418.2 4.6 %fusion.12 = f32[2560,256]{1,0:T(8,128)S(1)} fusion(f32[256,256]{1,0:T(8,128)S(1)} %fusion.171, f32[2560,128]{0,1:T(8,128)S(1)} %get-tuple-element.14, f32[2560,128]{0,1:T(8,128)S(1)} %get-tuple-element.13), kind=kOutput, calls=%fused_computation.80 | convolution fusion | flops 2013921280 | bytes 5505024 | tf_op jit(solution)/shard_map/dot_general | solution.py:69
  422.8 0.8 slice.59
  423.6 1.6 multiply_reduce_fusion
  425.2 5.7 %psum.39 = f32[256]{0:T(256)S(1)} all-reduce(f32[256]{0:T(256)S(1)} %get-tuple-element.3), channel_id=1, replica_groups=mesh['pair'=8,'row'=4] {'row'}, use_global_device_ids=true, to_apply=%region_9.10 | all-reduce | flops 256 | bytes 2048 | tf_op jit(solution)/shard_map/psum | solution.py:81
  430.9 0.6 add_sqrt_fusion
  (167 shorter events, 51.6 us)
Async XLA Ops:
  7.2 6.7 %copy-start.9 = (s32[16]{0:T(128)S(1)}, s32[16]{0:T(128)}, u32[]{:S(2)}) copy-start(s32[16]{0:T(128)} %param.3) | copy-start | bytes 196
  7.2 41.3 %all-reduce.5.cloned.1.call-start = ((), (), s32[]{:S(2)}) async-start(), calls=%async_computation | async-start | bytes 524288 | tf_op jit(solution)/shard_map/psum | solution.py:66
  13.6 155.8 %all-reduce.7.cloned.1.call-start = ((), (), s32[]{:S(2)}) async-start(), calls=%async_computation.1 | async-start | bytes 524288 | tf_op jit(solution)/shard_map/psum | solution.py:66
  48.5 2.6 copy-start.5
  65.2 1.6 copy-start
  71.1 58.7 %collective-permute-start = (f32[2560,128]{0,1:T(8,128)}, f32[2560,128]{0,1:T(8,128)}, u32[]{:S(2)}, u32[]{:S(2)}) collective-permute-start(f32[2560,128]{0,1:T(8,128)} %get-tuple-element.23), channel_id=1, source_target_pairs={{0,4},{4,8},{8,12},{12,16},{16,20},{20,24},{24,28},{1,5},{5,9},{9,... | collective-permute-start | bytes 3932168 | tf_op jit(solution)/shard_map/ppermute | solution.py:14
  75.6 54.2 %collective-permute-start.1 = (f32[2560,128]{0,1:T(8,128)}, f32[2560,128]{0,1:T(8,128)}, u32[]{:S(2)}, u32[]{:S(2)}) collective-permute-start(f32[2560,128]{0,1:T(8,128)} %get-tuple-element.24), channel_id=1, source_target_pairs={{4,0},{8,4},{12,8},{16,12},{20,16},{24,20},{28,24},{5,1},{9,5},{13... | collective-permute-start | bytes 3932168 | tf_op jit(solution)/shard_map/ppermute | solution.py:14
  131.5 1.1 copy-start.1
  131.5 1.5 copy-start.3
  135.6 149.4 %all-reduce.9.cloned.1.call-start = ((), (), s32[]{:S(2)}) async-start(), calls=%async_computation.2 | async-start | bytes 524288 | tf_op jit(solution)/shard_map/psum | solution.py:66
  169.5 2.6 copy-start.6
  185.8 1.6 copy-start.4
  186.2 1.4 copy-start.2
  190.4 58.4 %collective-permute-start.2 = (f32[2560,128]{0,1:T(8,128)S(1)}, f32[2560,128]{0,1:T(8,128)S(1)}, u32[]{:S(2)}, u32[]{:S(2)}) collective-permute-start(f32[2560,128]{0,1:T(8,128)S(1)} %get-tuple-element.19), channel_id=1, source_target_pairs={{0,4},{4,8},{8,12},{12,16},{16,20},{20,24},{24,28},{1,5},{5,9},{9,... | collective-permute-start | bytes 3932168 | tf_op jit(solution)/shard_map/ppermute | solution.py:14
  193.9 54.9 %collective-permute-start.3 = (f32[2560,128]{0,1:T(8,128)S(1)}, f32[2560,128]{0,1:T(8,128)S(1)}, u32[]{:S(2)}, u32[]{:S(2)}) collective-permute-start(f32[2560,128]{0,1:T(8,128)S(1)} %get-tuple-element.20), channel_id=1, source_target_pairs={{4,0},{8,4},{12,8},{16,12},{20,16},{24,20},{28,24},{5,1},{9,5},{13... | collective-permute-start | bytes 3932168 | tf_op jit(solution)/shard_map/ppermute | solution.py:14
  251.6 148.8 %all-reduce.11.cloned.1.call-start = ((), (), s32[]{:S(2)}) async-start(), calls=%async_computation.3 | async-start | bytes 524288 | tf_op jit(solution)/shard_map/psum | solution.py:66
  285.0 2.6 copy-start.7
  305.7 58.4 %collective-permute-start.4 = (f32[2560,128]{0,1:T(8,128)S(1)}, f32[2560,128]{0,1:T(8,128)S(1)}, u32[]{:S(2)}, u32[]{:S(2)}) collective-permute-start(f32[2560,128]{0,1:T(8,128)S(1)} %get-tuple-element.15), channel_id=1, source_target_pairs={{0,4},{4,8},{8,12},{12,16},{16,20},{20,24},{24,28},{1,5},{5,9},{9,... | collective-permute-start | bytes 3932168 | tf_op jit(solution)/shard_map/ppermute | solution.py:14
  309.2 54.9 %collective-permute-start.5 = (f32[2560,128]{0,1:T(8,128)S(1)}, f32[2560,128]{0,1:T(8,128)S(1)}, u32[]{:S(2)}, u32[]{:S(2)}) collective-permute-start(f32[2560,128]{0,1:T(8,128)S(1)} %get-tuple-element.16), channel_id=1, source_target_pairs={{4,0},{8,4},{12,8},{16,12},{20,16},{24,20},{28,24},{5,1},{9,5},{13... | collective-permute-start | bytes 3932168 | tf_op jit(solution)/shard_map/ppermute | solution.py:14
  400.4 2.6 copy-start.8
Sparse Core Ops, SparseCore 0:
  13.8 34.6 all-reduce.4
  135.7 33.6 all-reduce.6
  251.7 33.2 all-reduce.8
  367.0 33.2 all-reduce.10
where the time goes:
time: 442 us; the launch traced here: 438 us
  waiting for transfers between devices  294 us (67%)
  matrix products  80.3 us (18%)
  between operations  18.1 us (4%)
  starting transfers between devices  16.4 us (4%)
  local copies, waits for them, and re-layouts  13.6 us (3%)
  other arithmetic  9.97 us (2%)
  blocking collectives  5.73 us (1%)
    ppermute x6, waiting for transfers between devices, from_behind(): return lax.ppermute(block, axis, route)  160 us
    psum x4, waiting for transfers between devices, per_device(): lax.psum(jnp.dot(columns.T, columns, precision=highest), 'row')  134 us
    dot_general x64, matrix products, rotation_of(): jnp.dot(inverse, 2.0 * identity - jnp.dot(system, inverse, precision=high...  24.9 us
    dot_general x64, matrix products, rotation_of(): jnp.dot(system, inverse, precision=highest)  24.2 us
    ppermute x6, starting transfers between devices, from_behind(): return lax.ppermute(block, axis, route)  15.2 us
    dot_general x4, matrix products, per_device(): jnp.dot(columns.T, columns, precision=highest)  14.1 us
    gather x4, local copies, waits for them, and re-layouts, rotation_of(): diagonal = jnp.diagonal(gram_matrix)  10.5 us
  transfers between devices with their start and end apart: 10, of which 7 were waited for; matrix products, arithmetic and copies ran while one was open for 0% of the time, Pallas kernels for 0%

commit v1 on v0

--- a/solution.py
+++ b/solution.py
@@ -63,7 +63,9 @@
     is_last = position == pair_count - 1
     for sweep_round in range(ROUNDS):
         columns = stacked[:local_rows]
-        gram_matrix = lax.psum(jnp.dot(columns.T, columns, precision=highest), "row")
+        block_2 = jnp.dot(columns.T, columns, precision=highest)
+        parts = lax.all_gather(block_2, "row")
+        gram_matrix = jnp.sum(parts, axis=0)
         rotation = rotation_of(gram_matrix)
         if sweep_round == ROUNDS - 1:
             stacked = jnp.dot(stacked, rotation, precision=highest)

time: 442 us -> 390 us (0.88)
  waiting for transfers between devices: 294 us -> 238 us
  other arithmetic: 9.97 us -> 15.2 us
    psum x4 -> x0, waiting for transfers between devices: 134 us -> none  [per_device(): lax.psum(jnp.dot(columns.T, columns, precision=highest), 'row')]
    all_gather x0 -> x4, waiting for transfers between devices: none -> 73.2 us  [per_device(): parts = lax.all_gather(block_2, 'row')]
    reduce_sum x0 -> x4, other arithmetic: none -> 5.31 us  [per_device(): gram_matrix = jnp.sum(parts, axis=0)]
    ppermute x6, waiting for transfers between devices: 160 us -> 165 us  [from_behind(): return lax.ppermute(block, axis, route)]
where the time goes in v1:
time: 390 us; the launch traced here: 386 us
  waiting for transfers between devices  238 us (61%)
  matrix products  80.5 us (21%)
  between operations  18.1 us (5%)
  starting transfers between devices  15.4 us (4%)
  other arithmetic  15.2 us (4%)
  local copies, waits for them, and re-layouts  13 us (3%)
  blocking collectives  5.86 us (2%)
    ppermute x6, waiting for transfers between devices, from_behind(): return lax.ppermute(block, axis, route)  165 us
    all_gather x4, waiting for transfers between devices, per_device(): parts = lax.all_gather(block_2, 'row')  73.2 us
    dot_general x64, matrix products, rotation_of(): jnp.dot(system, inverse, precision=highest)  25.2 us
    dot_general x64, matrix products, rotation_of(): jnp.dot(inverse, 2.0 * identity - jnp.dot(system, inverse, precision=high...  24.1 us
    ppermute x6, starting transfers between devices, from_behind(): return lax.ppermute(block, axis, route)  15.2 us
    dot_general x4, matrix products, per_device(): block_2 = jnp.dot(columns.T, columns, precision=highest)  14.1 us
    gather x4, local copies, waits for them, and re-layouts, rotation_of(): diagonal = jnp.diagonal(gram_matrix)  10.5 us
    dot_general x3, matrix products, per_device(): turned = jnp.dot(stacked, rotation, precision=highest)  7.87 us
  transfers between devices with their start and end apart: 10, of which 7 were waited for; matrix products, arithmetic and copies ran while one was open for 0% of the time, Pallas kernels for 0%

profile of v1, /device:TPU:0, one launch (start us, length us, event | category | flops | bytes accessed | tf_op | source)
XLA Modules:
  0.0 386.0 jit_solution(17600428581968654523)
XLA Ops:
  7.2 6.4 %fusion.107 = f32[256,256]{1,0:T(8,128)} fusion(f32[2048,256]{1,0:T(8,128)} %param.2), kind=kOutput, calls=%fused_computation.216 | convolution fusion | flops 1610612736 | bytes 2359296 | tf_op jit(solution)/shard_map/dot_general | solution.py:66
  14.0 19.2 %all-gather.9.cloned.1.call-done = f32[1024,256]{1,0:T(8,128)} async-done(((f32[256,256]{1,0:T(8,128)}), f32[1024,256]{1,0:T(8,128)}) %all-gather.9.cloned.1.call-update) | async-done | bytes 1048592 | tf_op jit(solution)/shard_map/all_gather | solution.py:67
  33.2 1.3 reduce_sum.81
  34.5 2.9 gather_fusion
  37.4 0.8 multiply_reduce_fusion.4
  38.6 0.4 fusion.56
  51.3 0.6 select_subtract_fusion.48
  52.9 2.6 fusion
  55.5 1.7 slice_select_fusion.8
  57.2 4.4 %collective-permute-start = (f32[2560,128]{0,1:T(8,128)}, f32[2560,128]{0,1:T(8,128)}, u32[]{:S(2)}, u32[]{:S(2)}) collective-permute-start(f32[2560,128]{0,1:T(8,128)} %get-tuple-element.23), channel_id=1, source_target_pairs={{0,4},{4,8},{8,12},{12,16},{16,20},{20,24},{24,28},{1,5},{5,9},{9,... | collective-permute-start | bytes 3932168 | tf_op jit(solution)/shard_map/ppermute | solution.py:14
  61.6 1.3 collective-permute-start.1
  62.9 54.5 %collective-permute-done = f32[2560,128]{0,1:T(8,128)} collective-permute-done((f32[2560,128]{0,1:T(8,128)}, f32[2560,128]{0,1:T(8,128)}, u32[]{:S(2)}, u32[]{:S(2)}) %collective-permute-start) | collective-permute-done | bytes 1310752 | tf_op jit(solution)/shard_map/ppermute | solution.py:14
  117.4 1.7 slice_select_fusion.7
  119.1 1.0 copy-done.1
  120.2 0.4 copy-done.3
  120.6 2.6 fusion.24
  123.2 18.2 %all-gather.11.cloned.1.call-done = f32[1024,256]{1,0:T(8,128)} async-done(((f32[256,256]{1,0:T(8,128)}), f32[1024,256]{1,0:T(8,128)}) %all-gather.11.cloned.1.call-update) | async-done | bytes 1048592 | tf_op jit(solution)/shard_map/all_gather | solution.py:67
  141.5 1.3 reduce_sum.83
  142.8 2.3 gather_fusion.1
  145.1 0.8 multiply_reduce_fusion.3
  146.3 0.4 fusion.57
  159.0 0.8 select_subtract_fusion.32
  160.6 2.6 fusion.4
  163.5 3.5 collective-permute-start.2
  166.9 1.3 collective-permute-start.3
  168.2 55.1 %collective-permute-done.2 = f32[2560,128]{0,1:T(8,128)S(1)} collective-permute-done((f32[2560,128]{0,1:T(8,128)S(1)}, f32[2560,128]{0,1:T(8,128)S(1)}, u32[]{:S(2)}, u32[]{:S(2)}) %collective-permute-start.2) | collective-permute-done | bytes 1310752 | tf_op jit(solution)/shard_map/ppermute | solution.py:14
  223.6 2.6 fusion.20
  226.2 17.8 %all-gather.13.cloned.1.call-done = f32[1024,256]{1,0:T(8,128)} async-done(((f32[256,256]{1,0:T(8,128)}), f32[1024,256]{1,0:T(8,128)}) %all-gather.13.cloned.1.call-update) | async-done | bytes 1048592 | tf_op jit(solution)/shard_map/all_gather | solution.py:67
  244.1 1.3 reduce_sum.85
  245.4 2.5 gather_fusion.2
  247.9 0.8 multiply_reduce_fusion.2
  249.1 0.4 fusion.58
  261.8 0.6 select_subtract_fusion.16
  263.2 2.6 fusion.8
  266.0 3.5 collective-permute-start.4
  269.5 1.3 collective-permute-start.5
  270.8 55.1 %collective-permute-done.4 = f32[2560,128]{0,1:T(8,128)S(1)} collective-permute-done((f32[2560,128]{0,1:T(8,128)S(1)}, f32[2560,128]{0,1:T(8,128)S(1)}, u32[]{:S(2)}, u32[]{:S(2)}) %collective-permute-start.4) | collective-permute-done | bytes 1310752 | tf_op jit(solution)/shard_map/ppermute | solution.py:14
  326.1 2.6 fusion.16
  328.7 17.9 %all-gather.15.cloned.1.call-done = f32[1024,256]{1,0:T(8,128)} async-done(((f32[256,256]{1,0:T(8,128)}), f32[1024,256]{1,0:T(8,128)}) %all-gather.15.cloned.1.call-update) | async-done | bytes 1048592 | tf_op jit(solution)/shard_map/all_gather | solution.py:67
  346.6 1.3 reduce_sum.87
  348.0 2.7 gather_fusion.3
  350.7 0.8 multiply_reduce_fusion.1
  364.6 0.6 select_subtract_fusion
  365.9 4.6 %fusion.12 = f32[2560,256]{1,0:T(8,128)S(1)} fusion(f32[256,256]{1,0:T(8,128)S(1)} %fusion.171, f32[2560,128]{0,1:T(8,128)S(1)} %get-tuple-element.14, f32[2560,128]{0,1:T(8,128)S(1)} %get-tuple-element.13), kind=kOutput, calls=%fused_computation.80 | convolution fusion | flops 2013921280 | bytes 5505024 | tf_op jit(solution)/shard_map/dot_general | solution.py:71
  370.5 0.8 slice.59
  371.3 1.6 multiply_reduce_fusion
  372.9 5.9 %psum.7 = f32[256]{0:T(256)S(1)} all-reduce(f32[256]{0:T(256)S(1)} %get-tuple-element.3), channel_id=1, replica_groups=mesh['pair'=8,'row'=4] {'row'}, use_global_device_ids=true, to_apply=%region_9.10 | all-reduce | flops 256 | bytes 2048 | tf_op jit(solution)/shard_map/psum | solution.py:83
  378.7 0.6 add_sqrt_fusion
  (163 shorter events, 51.9 us)
Async XLA Ops:
  7.2 6.5 %copy-start.5 = (s32[16]{0:T(128)S(1)}, s32[16]{0:T(128)}, u32[]{:S(2)}) copy-start(s32[16]{0:T(128)} %param.3) | copy-start | bytes 196
  7.2 26.0 %all-gather.9.cloned.1.call-start = ((), (), s32[]{:S(2)}) async-start(), calls=%async_computation | async-start | bytes 1310720 | tf_op jit(solution)/shard_map/all_gather | solution.py:67
  13.6 127.8 %all-gather.11.cloned.1.call-start = ((), (), s32[]{:S(2)}) async-start(), calls=%async_computation.1 | async-start | bytes 1310720 | tf_op jit(solution)/shard_map/all_gather | solution.py:67
  51.3 1.6 copy-start
  57.2 60.2 %collective-permute-start = (f32[2560,128]{0,1:T(8,128)}, f32[2560,128]{0,1:T(8,128)}, u32[]{:S(2)}, u32[]{:S(2)}) collective-permute-start(f32[2560,128]{0,1:T(8,128)} %get-tuple-element.23), channel_id=1, source_target_pairs={{0,4},{4,8},{8,12},{12,16},{16,20},{20,24},{24,28},{1,5},{5,9},{9,... | collective-permute-start | bytes 3932168 | tf_op jit(solution)/shard_map/ppermute | solution.py:14
  61.6 55.8 %collective-permute-start.1 = (f32[2560,128]{0,1:T(8,128)}, f32[2560,128]{0,1:T(8,128)}, u32[]{:S(2)}, u32[]{:S(2)}) collective-permute-start(f32[2560,128]{0,1:T(8,128)} %get-tuple-element.24), channel_id=1, source_target_pairs={{4,0},{8,4},{12,8},{16,12},{20,16},{24,20},{28,24},{5,1},{9,5},{13... | collective-permute-start | bytes 3932168 | tf_op jit(solution)/shard_map/ppermute | solution.py:14
  119.1 1.1 copy-start.1
  119.1 1.5 copy-start.3
  123.2 120.9 %all-gather.13.cloned.1.call-start = ((), (), s32[]{:S(2)}) async-start(), calls=%async_computation.2 | async-start | bytes 1310720 | tf_op jit(solution)/shard_map/all_gather | solution.py:67
  158.6 2.0 copy-start.4
  159.0 1.6 copy-start.2
  163.5 59.9 %collective-permute-start.2 = (f32[2560,128]{0,1:T(8,128)S(1)}, f32[2560,128]{0,1:T(8,128)S(1)}, u32[]{:S(2)}, u32[]{:S(2)}) collective-permute-start(f32[2560,128]{0,1:T(8,128)S(1)} %get-tuple-element.19), channel_id=1, source_target_pairs={{0,4},{4,8},{8,12},{12,16},{16,20},{20,24},{24,28},{1,5},{5,9},{9,... | collective-permute-start | bytes 3932168 | tf_op jit(solution)/shard_map/ppermute | solution.py:14
  166.9 56.4 %collective-permute-start.3 = (f32[2560,128]{0,1:T(8,128)S(1)}, f32[2560,128]{0,1:T(8,128)S(1)}, u32[]{:S(2)}, u32[]{:S(2)}) collective-permute-start(f32[2560,128]{0,1:T(8,128)S(1)} %get-tuple-element.20), channel_id=1, source_target_pairs={{4,0},{8,4},{12,8},{16,12},{20,16},{24,20},{28,24},{5,1},{9,5},{13... | collective-permute-start | bytes 3932168 | tf_op jit(solution)/shard_map/ppermute | solution.py:14
  226.2 120.4 %all-gather.15.cloned.1.call-start = ((), (), s32[]{:S(2)}) async-start(), calls=%async_computation.3 | async-start | bytes 1310720 | tf_op jit(solution)/shard_map/all_gather | solution.py:67
  266.0 59.9 %collective-permute-start.4 = (f32[2560,128]{0,1:T(8,128)S(1)}, f32[2560,128]{0,1:T(8,128)S(1)}, u32[]{:S(2)}, u32[]{:S(2)}) collective-permute-start(f32[2560,128]{0,1:T(8,128)S(1)} %get-tuple-element.15), channel_id=1, source_target_pairs={{0,4},{4,8},{8,12},{12,16},{16,20},{20,24},{24,28},{1,5},{5,9},{9,... | collective-permute-start | bytes 3932168 | tf_op jit(solution)/shard_map/ppermute | solution.py:14
  269.5 56.4 %collective-permute-start.5 = (f32[2560,128]{0,1:T(8,128)S(1)}, f32[2560,128]{0,1:T(8,128)S(1)}, u32[]{:S(2)}, u32[]{:S(2)}) collective-permute-start(f32[2560,128]{0,1:T(8,128)S(1)} %get-tuple-element.16), channel_id=1, source_target_pairs={{4,0},{8,4},{12,8},{16,12},{20,16},{24,20},{28,24},{5,1},{9,5},{13... | collective-permute-start | bytes 3932168 | tf_op jit(solution)/shard_map/ppermute | solution.py:14
Sparse Core Ops, SparseCore 0:
  13.8 19.4 all-gather.8
  123.3 18.1 all-gather.10
  226.3 17.7 all-gather.12
  328.9 17.7 all-gather.14
